TPU v7x, 512 devices: a whole 4x4x16 slice. The times are simulated.
512 devices in a mesh: wide: 64 (over z, x), narrow: 8 (over y, core).
Axes of the slice: x: 4, y: 4, z: 16, core: 2. Of those that a mesh axis runs over, the one named last changes fastest.
Arguments:
- sublevel_symbol_entries: bfloat16 [1024, 4, 4096], P('wide', None, 'narrow'), may hold values from -160 to 160
- prior_symbol_memory: bfloat16 [1024, 4096], P('wide', 'narrow'), may hold values from -6 to 6
- entry_scaling_multiplier: float32 [4096], P('narrow'), may hold values from 0.25 to 1.75
- entry_scaling_offset: float32 [4096], P('narrow'), may hold values from -4 to 4
- learned_blending: float32 [6, 4096], P(None, 'narrow'), may hold values from 0 to 1
- blending_lowering_coefficients: bfloat16 [4096, 160], P('narrow'), may hold values from -0.09375 to 0.09375
- blending_raising_coefficients: bfloat16 [5, 32, 4096], P(None, None, 'narrow'), may hold values from -1 to 1
- fading_lowering_coefficients: bfloat16 [4096, 64], P('narrow'), may hold values from -0.09375 to 0.09375
- fading_raising_coefficients: bfloat16 [64, 4096], P(None, 'wide'), may hold values from -0.75 to 0.75
- learned_fading: float32 [4096], P('wide'), may hold values from -6 to 1
- immediate_item_premium: float32 [4096], P('wide'), may hold values from -3 to 3
- acceptor_projection: bfloat16 [4096, 4096], P('narrow', 'wide'), may hold values from -0.09375 to 0.09375
- lookup_projection: bfloat16 [4096, 4096], P('narrow', 'wide'), may hold values from -0.09375 to 0.09375
- payload_projection: bfloat16 [4096, 4096], P('narrow', 'wide'), may hold values from -0.09375 to 0.09375
- gating_projection: bfloat16 [4096, 4096], P('narrow', 'wide'), may hold values from -0.09375 to 0.09375
- emission_projection: bfloat16 [4096, 4096], P(None, 'wide'), may hold values from -0.09375 to 0.09375
- group_scaling_multiplier: float32 [4096], P('wide'), may hold values from 0.25 to 1.75
- group_scaling_offset: float32 [4096], P('wide'), may hold values from -4 to 4
- dialogue_group_memory: float32 [262144, 1024], P('wide', 'narrow'), may hold values from -6 to 6
Outputs:
- mixing_output: bfloat16 [1024, 4, 4096], P('narrow', None, 'wide')
- final_state: float32 [262144, 1024], P('wide', 'narrow')
All inputs are finite; a program needn't handle non-finite values.
Results may differ from a plain program's by a relative error of at most 0.034.
Values may be sent and summed in bfloat16 or wider, within the bound.
A program may use at most 64 MiB of HBM per device.

v0:
```python
import jax
import jax.numpy as jnp
from jax import lax
from jax.sharding import PartitionSpec as P

CHANNEL_SPAN = 64
FEATURE_EXTENT = 4096


def per_device(
    sublevel_symbol_entries,
    prior_symbol_memory,
    entry_scaling_multiplier,
    entry_scaling_offset,
    learned_blending,
    blending_lowering_coefficients,
    blending_raising_coefficients,
    fading_lowering_coefficients,
    fading_raising_coefficients,
    learned_fading,
    immediate_item_premium,
    acceptor_projection,
    lookup_projection,
    payload_projection,
    gating_projection,
    emission_projection,
    group_scaling_multiplier,
    group_scaling_offset,
    dialogue_group_memory,
):
    rank = blending_raising_coefficients.shape[1]
    narrow_rows = dialogue_group_memory.shape[1]
    local_width = emission_projection.shape[1]
    group_partition = local_width // CHANNEL_SPAN
    weights = (acceptor_projection, lookup_projection, payload_projection, gating_projection)
    shift_gathered = lax.all_gather(prior_symbol_memory, "wide", axis=0, tiled=True)

    def channel_set_first(block):
        return block.reshape(narrow_rows, group_partition, CHANNEL_SPAN).transpose(1, 2, 0)

    present_symbol = dialogue_group_memory.reshape(
        group_partition, CHANNEL_SPAN, CHANNEL_SPAN, narrow_rows
    )
    previous_rows = prior_symbol_memory
    previous_all = shift_gathered
    results = []
    for index in range(sublevel_symbol_entries.shape[1]):
        floats = sublevel_symbol_entries[:, index : index + 1].astype(jnp.float32)
        totals, squares = lax.psum((jnp.sum(floats, -1), jnp.sum(floats * floats, -1)), "narrow")
        prepare_center = totals[..., None] / FEATURE_EXTENT
        spread = squares[..., None] / FEATURE_EXTENT - prepare_center * prepare_center
        normed = (
            (floats - prepare_center) * lax.rsqrt(spread + 1e-05) * entry_scaling_multiplier
            + entry_scaling_offset
        ).astype(jnp.bfloat16)
        previous = jnp.concatenate([previous_rows[:, None], normed[:, :-1]], 1)
        prepare_normalized_float = normed.astype(jnp.float32)
        prepare_shifted_input = previous.astype(jnp.float32) - prepare_normalized_float
        blended = (prepare_normalized_float + prepare_shifted_input * learned_blending[0]).astype(
            jnp.bfloat16
        )
        partial_mix = jnp.einsum(
            "smd,dr->smr",
            blended,
            blending_lowering_coefficients,
            preferred_element_type=jnp.float32,
        )
        hidden_activation = jnp.tanh(lax.psum(partial_mix, "narrow")).astype(jnp.bfloat16)
        decay_shift = jnp.einsum(
            "smr,rd->smd",
            hidden_activation[..., :rank],
            blending_raising_coefficients[0],
            preferred_element_type=jnp.float32,
        )
        decay_mix = (
            prepare_normalized_float + prepare_shifted_input * (learned_blending[1] + decay_shift)
        ).astype(jnp.bfloat16)
        partial_decay = jnp.einsum(
            "smd,dr->smr",
            decay_mix,
            fading_lowering_coefficients,
            preferred_element_type=jnp.float32,
        )
        decay_hidden = jnp.tanh(lax.psum(partial_decay, "narrow")).astype(jnp.bfloat16)
        small = jnp.concatenate([hidden_activation[..., rank:], decay_hidden], -1)
        prepare_normed_all = lax.all_gather(normed, "wide", axis=0, tiled=True)
        prepare_small_all = lax.all_gather(small, "wide", axis=0, tiled=True)
        normed, normed_all, small_all = (normed, prepare_normed_all, prepare_small_all)
        project_previous_all = previous_all[:, None]
        normalized_float = normed_all.astype(jnp.float32)
        shifted_input = project_previous_all.astype(jnp.float32) - normalized_float
        term_results = []
        for selector_index in range(4):
            low_rank_update = jnp.einsum(
                "smr,rd->smd",
                small_all[..., selector_index * rank : (selector_index + 1) * rank],
                blending_raising_coefficients[selector_index + 1],
                preferred_element_type=jnp.float32,
            )
            mixed_input = (
                normalized_float
                + shifted_input * (learned_blending[selector_index + 2] + low_rank_update)
            ).astype(jnp.bfloat16)
            term_results.append(
                jnp.einsum(
                    "smd,de->sme",
                    mixed_input,
                    weights[selector_index],
                    preferred_element_type=jnp.float32,
                )
            )
        project_transformed_outcome = lax.psum_scatter(
            jnp.concatenate(term_results, -1).astype(jnp.bfloat16),
            "narrow",
            scatter_dimension=0,
            tiled=True,
        ).astype(jnp.float32)
        rows_start = lax.axis_index("narrow") * narrow_rows
        decay_rows = lax.dynamic_slice_in_dim(
            small_all[..., 4 * rank :], rows_start, narrow_rows, 0
        )
        decay_log = learned_fading + jnp.einsum(
            "smr,rd->smd",
            decay_rows,
            fading_raising_coefficients,
            preferred_element_type=jnp.float32,
        )
        shrink_coefficient = jnp.exp(-jnp.exp(decay_log))
        recurrence_present_symbol = present_symbol
        each_group_reward = immediate_item_premium.reshape(group_partition, CHANNEL_SPAN)
        present_acceptor = channel_set_first(project_transformed_outcome[:, 0, :local_width])
        key_now = channel_set_first(
            project_transformed_outcome[:, 0, local_width : 2 * local_width]
        )
        value_now = channel_set_first(
            project_transformed_outcome[:, 0, 2 * local_width : 3 * local_width]
        )
        gate_now = project_transformed_outcome[:, 0, 3 * local_width :]
        forget_now = channel_set_first(shrink_coefficient[:, 0])
        dyadic_tensor = key_now[:, :, None, :] * value_now[:, None, :, :]
        memory_retrieval = jnp.sum(
            present_acceptor[:, :, None, :]
            * (recurrence_present_symbol + each_group_reward[:, :, None, None] * dyadic_tensor),
            1,
        )
        recurrence_present_symbol = (
            forget_now[:, :, None, :] * recurrence_present_symbol + dyadic_tensor
        )
        center = jnp.mean(memory_retrieval, 1, keepdims=True)
        offset = memory_retrieval - center
        scaled = offset * lax.rsqrt(jnp.mean(offset * offset, 1, keepdims=True) + 0.00064)
        squashed_vector = scaled.transpose(2, 0, 1).reshape(narrow_rows, local_width)
        pieces = [
            (
                (squashed_vector * group_scaling_multiplier + group_scaling_offset)
                * jax.nn.silu(gate_now)
            ).astype(jnp.bfloat16)
        ]
        present_symbol = recurrence_present_symbol
        gated = jnp.stack(pieces, 1)
        results.append(
            jnp.einsum(
                "smc,ce->sme",
                lax.all_gather(gated, "wide", axis=2, tiled=True),
                emission_projection,
                preferred_element_type=jnp.float32,
            ).astype(jnp.bfloat16)
        )
        previous_rows = normed[:, 0]
        previous_all = normed_all[:, 0]
    mixing_output = jnp.concatenate(results, 1)
    return (
        mixing_output,
        present_symbol.reshape(group_partition * CHANNEL_SPAN * CHANNEL_SPAN, narrow_rows),
    )


def solution(mesh):
    placed = (
        P("wide", None, "narrow"),
        P("wide", "narrow"),
        P("narrow"),
        P("narrow"),
        P(None, "narrow"),
        P("narrow", None),
        P(None, None, "narrow"),
        P("narrow", None),
        P(None, "wide"),
        P("wide"),
        P("wide"),
        P("narrow", "wide"),
        P("narrow", "wide"),
        P("narrow", "wide"),
        P("narrow", "wide"),
        P(None, "wide"),
        P("wide"),
        P("wide"),
        P("wide", "narrow"),
    )
    return jax.shard_map(
        per_device,
        mesh=mesh,
        in_specs=placed,
        out_specs=(P("narrow", None, "wide"), P("wide", "narrow")),
        check_vma=False,
    )
```

profile of v0, /device:TPU:8, one launch (start us, length us, event | category | flops | bytes accessed | tf_op | source)
XLA Modules:
  0.0 1447.9 jit_solution(15403730953367358589)
XLA Ops:
  8.7 14.8 %all-reduce.2 = (f32[16,1]{0,1:T(1,128)S(1)}, f32[16,1]{0,1:T(1,128)S(1)}, f32[16,1]{0,1:T(1,128)S(1)}, f32[16,1]{0,1:T(1,128)S(1)}, f32[16,1]{0,1:T(1,128)S(1)}...) all-reduce(f32[16,1]{0,1:T(1,128)S(1)} %bitcast.846, ...), channel_id=1, replica_groups=mesh['wide'=64,'narrow'=8] {'narrow'}, use_global_device_ids=true, to_apply=%region_13.14 | all-reduce | flops 128 | bytes 1024 | tf_op jit(solution)/shard_map/psum | solution.py:49
  33.1 24.0 %all-reduce.1 = (f32[16,1,160]{2,0,1:T(8,128)S(1)}, f32[16,1,160]{2,0,1:T(8,128)S(1)}, f32[16,1,160]{2,0,1:T(8,128)S(1)}, f32[16,1,160]{2,0,1:T(8,128)S(1)}) all-reduce(f32[16,1,160]{2,0,1:T(8,128)S(1)} %convolution_bitcast_fusion.1, ...), channel_id=1, replica_groups=mesh['wide'=64,'narrow'=8] {'narrow'}, use_global_device_ids=true, to_apply=%region_24.25 | all-reduce | flops 10240 | bytes 81920 | tf_op jit(solution)/shard_map/psum | solution.py:68
  61.9 24.4 %all-reduce = (f32[16,1,64]{2,0,1:T(8,128)S(1)}, f32[16,1,64]{2,0,1:T(8,128)S(1)}, f32[16,1,64]{2,0,1:T(8,128)S(1)}, f32[16,1,64]{2,0,1:T(8,128)S(1)}) all-reduce(f32[16,1,64]{2,0,1:T(8,128)S(1)} %convolution_bitcast_fusion.5, f32[16,1,64]{2,0,1:T(8,128)S(1)} %convolution_bitcast_fusion.6, ...), channel_id=1, replica_groups=mesh['wide'=64,'narrow'=8] {'narrow'}, use_global_device_ids=true, to_apply=%region_25.26 | all-reduce | flops 4096 | bytes 32768 | tf_op jit(solution)/shard_map/psum | solution.py:84
  86.4 103.3 %all_gather.50 = bf16[1024,1,192]{2,0,1:T(8,128)(2,1)S(1)} all-gather(bf16[16,1,192]{2,0,1:T(8,128)(2,1)S(1)} %pad_maximum_fusion.4), channel_id=1, replica_groups=mesh['wide'=64,'narrow'=8] {'wide'}, dimensions={0}, use_global_device_ids=true | all-gather | bytes 399360 | tf_op jit(solution)/shard_map/all_gather | solution.py:87
  189.7 99.2 %all_gather.41 = bf16[1024,1,192]{2,0,1:T(8,128)(2,1)S(1)} all-gather(bf16[16,1,192]{2,0,1:T(8,128)(2,1)S(1)} %pad_maximum_fusion.1), channel_id=1, replica_groups=mesh['wide'=64,'narrow'=8] {'wide'}, dimensions={0}, use_global_device_ids=true | all-gather | bytes 399360 | tf_op jit(solution)/shard_map/all_gather | solution.py:87
  288.9 97.0 %all_gather.44 = bf16[1024,1,192]{2,0,1:T(8,128)(2,1)S(1)} all-gather(bf16[16,1,192]{2,0,1:T(8,128)(2,1)S(1)} %pad_maximum_fusion.2), channel_id=1, replica_groups=mesh['wide'=64,'narrow'=8] {'wide'}, dimensions={0}, use_global_device_ids=true | all-gather | bytes 399360 | tf_op jit(solution)/shard_map/all_gather | solution.py:87
  385.9 99.0 %all_gather.47 = bf16[1024,1,192]{2,0,1:T(8,128)(2,1)S(1)} all-gather(bf16[16,1,192]{2,0,1:T(8,128)(2,1)S(1)} %pad_maximum_fusion.3), channel_id=1, replica_groups=mesh['wide'=64,'narrow'=8] {'wide'}, dimensions={0}, use_global_device_ids=true | all-gather | bytes 399360 | tf_op jit(solution)/shard_map/all_gather | solution.py:87
  487.3 2.4 fusion.75
  489.7 2.4 fusion.74
  492.2 2.3 fusion.73
  498.1 81.7 %all-gather.10.cloned.1.call-done = bf16[1024,1,512]{2,0,1:T(8,128)(2,1)} async-done(((bf16[16,1,512]{2,0,1:T(8,128)(2,1)}), bf16[1024,1,512]{2,0,1:T(8,128)(2,1)}) %all-gather.10.cloned.1.call-update) | async-done | bytes 1048592 | tf_op jit(solution)/shard_map/all_gather | solution.py:86
  579.9 2.4 fusion.63
  582.3 2.4 fusion.62
  584.7 2.4 fusion.61
  590.5 127.2 %all-gather.16.cloned.1.call-done = bf16[1024,1,512]{2,0,1:T(8,128)(2,1)} async-done(((bf16[16,1,512]{2,0,1:T(8,128)(2,1)}), bf16[1024,1,512]{2,0,1:T(8,128)(2,1)}) %all-gather.16.cloned.1.call-update) | async-done | bytes 1048592 | tf_op jit(solution)/shard_map/all_gather | solution.py:86
  717.7 2.4 fusion.67
  737.2 14.9 %reduce-scatter.19.cloned.1.call-done = bf16[128,256]{1,0:T(8,128)(2,1)} async-done(((bf16[1024,256]{1,0:T(8,128)(2,1)}), bf16[128,256]{1,0:T(8,128)(2,1)}) %reduce-scatter.19.cloned.1.call-update) | async-done | bytes 65552
  753.0 39.6 %reduce-scatter.13.cloned.1.call-done = bf16[128,256]{1,0:T(8,128)(2,1)} async-done(((bf16[1024,256]{1,0:T(8,128)(2,1)}), bf16[128,256]{1,0:T(8,128)(2,1)}) %reduce-scatter.13.cloned.1.call-update) | async-done | bytes 65552
  793.6 39.4 %reduce-scatter.15.cloned.1.call-done = bf16[128,256]{1,0:T(8,128)(2,1)} async-done(((bf16[1024,256]{1,0:T(8,128)(2,1)}), bf16[128,256]{1,0:T(8,128)(2,1)}) %reduce-scatter.15.cloned.1.call-update) | async-done | bytes 65552
  834.0 40.1 %reduce-scatter.17.cloned.1.call-done = bf16[128,256]{1,0:T(8,128)(2,1)} async-done(((bf16[1024,256]{1,0:T(8,128)(2,1)}), bf16[128,256]{1,0:T(8,128)(2,1)}) %reduce-scatter.17.cloned.1.call-update) | async-done | bytes 65552
  886.4 138.9 %all-gather.14.cloned.1.call-done = bf16[128,1,4096]{0,2,1:T(8,128)(2,1)} async-done(((bf16[128,1,64]{0,2,1:T(8,128)(2,1)}), bf16[128,1,4096]{0,2,1:T(8,128)(2,1)}) %all-gather.14.cloned.1.call-update) | async-done | bytes 1048592 | tf_op jit(solution)/shard_map/all_gather | solution.py:164
  1026.9 136.4 %all-gather.18.cloned.1.call-done = bf16[128,1,4096]{0,2,1:T(8,128)(2,1)} async-done(((bf16[128,1,64]{0,2,1:T(8,128)(2,1)}), bf16[128,1,4096]{0,2,1:T(8,128)(2,1)}) %all-gather.18.cloned.1.call-update) | async-done | bytes 1048592 | tf_op jit(solution)/shard_map/all_gather | solution.py:164
  1164.9 136.3 %all-gather.22.cloned.1.call-done = bf16[128,1,4096]{0,2,1:T(8,128)(2,1)} async-done(((bf16[128,1,64]{0,2,1:T(8,128)(2,1)}), bf16[128,1,4096]{0,2,1:T(8,128)(2,1)}) %all-gather.22.cloned.1.call-update) | async-done | bytes 1048592 | tf_op jit(solution)/shard_map/all_gather | solution.py:164
  1302.7 136.4 %all-gather.26.cloned.1.call-done = bf16[128,1,4096]{0,2,1:T(8,128)(2,1)} async-done(((bf16[128,1,64]{0,2,1:T(8,128)(2,1)}), bf16[128,1,4096]{0,2,1:T(8,128)(2,1)}) %all-gather.26.cloned.1.call-update) | async-done | bytes 1048592 | tf_op jit(solution)/shard_map/all_gather | solution.py:164
  (170 shorter events, 63.7 us)
Async XLA Ops:
  7.2 1018.2 %copy-start = (bf16[4096,64]{0,1:T(8,128)(2,1)S(1)}, bf16[4096,64]{0,1:T(8,128)(2,1)}, u32[]{:S(2)}) copy-start(bf16[4096,64]{0,1:T(8,128)(2,1)} %param.34) | copy-start | bytes 1572868
  7.2 52.3 %copy-start.4 = (bf16[16,512]{1,0:T(8,128)(2,1)S(1)}, bf16[16,512]{1,0:T(8,128)(2,1)}, u32[]{:S(2)}) copy-start(bf16[16,512]{1,0:T(8,128)(2,1)} %param.20) | copy-start | bytes 49156
  7.2 52.3 %copy-start.2 = (bf16[512,64]{0,1:T(8,128)(2,1)S(1)}, bf16[512,64]{0,1:T(8,128)(2,1)}, u32[]{:S(2)}) copy-start(bf16[512,64]{0,1:T(8,128)(2,1)} %param.26) | copy-start | bytes 196612
  7.2 54.5 %copy-start.7 = (f32[64]{0:T(128)S(1)}, f32[64]{0:T(128)}, u32[]{:S(2)}) copy-start(f32[64]{0:T(128)} %param.29) | copy-start | bytes 772
  7.2 480.1 %all-gather.24.cloned.1.call-start = ((), (), s32[]{:S(2)}) async-start(), calls=%async_computation.11 | async-start | bytes 1064960 | tf_op jit(solution)/shard_map/all_gather | solution.py:86
  25.0 462.3 %all-gather.20.cloned.1.call-start = ((), (), s32[]{:S(2)}) async-start(), calls=%async_computation.9 | async-start | bytes 1064960 | tf_op jit(solution)/shard_map/all_gather | solution.py:86
  25.7 472.4 %all-gather.12.cloned.1.call-start = ((), (), s32[]{:S(2)}) async-start(), calls=%async_computation.5 | async-start | bytes 1064960 | tf_op jit(solution)/shard_map/all_gather | solution.py:36
  26.5 553.4 %all-gather.10.cloned.1.call-start = ((), (), s32[]{:S(2)}) async-start(), calls=%async_computation.4 | async-start | bytes 1064960 | tf_op jit(solution)/shard_map/all_gather | solution.py:86
  27.1 690.7 %all-gather.16.cloned.1.call-start = ((), (), s32[]{:S(2)}) async-start(), calls=%async_computation.7 | async-start | bytes 1064960 | tf_op jit(solution)/shard_map/all_gather | solution.py:86
  27.6 724.4 %reduce-scatter.19.cloned.1.call-start = ((), (), s32[]{:S(2)}) async-start(), calls=%async_computation.16 | async-start | bytes 589824
  86.3 399.3 %copy-start.3 = (bf16[64,64]{1,0:T(8,128)(2,1)S(1)}, bf16[64,64]{1,0:T(8,128)(2,1)}, u32[]{:S(2)}) copy-start(bf16[64,64]{1,0:T(8,128)(2,1)} %param.27) | copy-start | bytes 24580
  86.4 399.3 %copy-start.6 = (f32[64]{0:T(128)S(1)}, f32[64]{0:T(128)}, u32[]{:S(2)}) copy-start(f32[64]{0:T(128)} %param.28) | copy-start | bytes 772
  489.7 2.5 copy-start.5
  489.7 2.5 copy-start.15
  497.8 84.4 %copy-start.13 = (bf16[512,64]{0,1:T(8,128)(2,1)S(1)}, bf16[512,64]{0,1:T(8,128)(2,1)}, u32[]{:S(2)}) copy-start(bf16[512,64]{0,1:T(8,128)(2,1)} %param.32) | copy-start | bytes 196612
  497.9 294.8 %reduce-scatter.13.cloned.1.call-start = ((), (), s32[]{:S(2)}) async-start(), calls=%async_computation.13 | async-start | bytes 589824
  589.4 128.4 %copy-start.12 = (bf16[512,64]{0,1:T(8,128)(2,1)S(1)}, bf16[512,64]{0,1:T(8,128)(2,1)}, u32[]{:S(2)}) copy-start(bf16[512,64]{0,1:T(8,128)(2,1)} %param.33) | copy-start | bytes 196612
  590.4 242.6 %reduce-scatter.15.cloned.1.call-start = ((), (), s32[]{:S(2)}) async-start(), calls=%async_computation.14 | async-start | bytes 589824
  717.7 2.5 copy-start.11
  727.3 146.8 %reduce-scatter.17.cloned.1.call-start = ((), (), s32[]{:S(2)}) async-start(), calls=%async_computation.15 | async-start | bytes 589824
  736.9 288.5 %all-gather.14.cloned.1.call-start = ((), (), s32[]{:S(2)}) async-start(), calls=%async_computation.6 | async-start | bytes 1064960 | tf_op jit(solution)/shard_map/all_gather | solution.py:164
  884.4 279.0 %all-gather.18.cloned.1.call-start = ((), (), s32[]{:S(2)}) async-start(), calls=%async_computation.8 | async-start | bytes 1064960 | tf_op jit(solution)/shard_map/all_gather | solution.py:164
  885.1 416.1 %all-gather.22.cloned.1.call-start = ((), (), s32[]{:S(2)}) async-start(), calls=%async_computation.10 | async-start | bytes 1064960 | tf_op jit(solution)/shard_map/all_gather | solution.py:164
  885.7 553.5 %all-gather.26.cloned.1.call-start = ((), (), s32[]{:S(2)}) async-start(), calls=%async_computation.12 | async-start | bytes 1064960 | tf_op jit(solution)/shard_map/all_gather | solution.py:164
  (9 other events, 18.9 us)
Sparse Core Ops, SparseCore 0:
  25.1 140.8 all-gather.23
  168.9 134.9 all-gather.19
  306.8 135.0 all-gather.11
  444.7 135.1 all-gather.9
  582.7 134.9 all-gather.15
  720.4 31.6 reduce-scatter.18
  755.1 37.5 reduce-scatter.12
  795.5 37.4 reduce-scatter.14
  836.6 37.5 reduce-scatter.16
  884.5 140.8 all-gather.13
  1028.3 134.9 all-gather.17
  1166.2 134.9 all-gather.21
  1304.1 134.9 all-gather.25
where the time goes:
time: 1450 us
  waiting for transfers between devices  896 us (62%)
  blocking collectives  462 us (32%)
  matrix products  51.9 us (4%)
  between operations  14.7 us (1%)
    all_gather x4, waiting for transfers between devices, per_device(): lax.all_gather(gated, 'wide', axis=2, tiled=True)  548 us
    all_gather x4, blocking collectives, per_device(): prepare_small_all = lax.all_gather(small, 'wide', axis=0, tiled=True)  398 us
    all_gather x4, waiting for transfers between devices, per_device(): prepare_normed_all = lax.all_gather(normed, 'wide', axis=0, tiled=True)  209 us
    unnamed x17, waiting for transfers between devices  138 us
    dot_general x16, matrix products, per_device(): jnp.einsum('smd,de->sme', mixed_input, weights[selector_index], preferred...  35.5 us
  transfers between devices with their start and end apart: 13, of which 10 were waited for; matrix products, arithmetic and copies ran while one was open for 4% of the time, Pallas kernels for 0%

commit v1 on v0

--- a/solution.py
+++ b/solution.py
@@ -161,7 +161,9 @@
         results.append(
             jnp.einsum(
                 "smc,ce->sme",
-                lax.all_gather(gated, "wide", axis=2, tiled=True),
+                jnp.concatenate(
+                    lax.all_to_all(jnp.stack([gated] * lax.axis_size("wide")), "wide", 0, 0), axis=2
+                ),
                 emission_projection,
                 preferred_element_type=jnp.float32,
             ).astype(jnp.bfloat16)

time: 1450 us -> 1140 us (0.79)
  the two profiles are of different devices: /device:TPU:8 before, /device:TPU:24 now
where the time goes in v1:
time: 1140 us
  blocking collectives  653 us (57%)
  waiting for transfers between devices  386 us (34%)
  matrix products  49.4 us (4%)
  local copies, waits for them, and re-layouts  16.1 us (1%)
  between operations  14.7 us (1%)
    all_gather x4, blocking collectives, per_device(): prepare_small_all = lax.all_gather(small, 'wide', axis=0, tiled=True)  398 us
    all_to_all x3, blocking collectives, per_device(): lax.all_to_all(jnp.stack([gated] * lax.axis_size('wide')), 'wide', 0, 0)  193 us
    all_gather x4, waiting for transfers between devices, per_device(): prepare_normed_all = lax.all_gather(normed, 'wide', axis=0, tiled=True)  187 us
    unnamed x13, waiting for transfers between devices  146 us
    all_to_all x1, waiting for transfers between devices, per_device(): lax.all_to_all(jnp.stack([gated] * lax.axis_size('wide')), 'wide', 0, 0)  52 us
    dot_general x16, matrix products, per_device(): jnp.einsum('smd,de->sme', mixed_input, weights[selector_index], preferred...  36.6 us
    psum x1, blocking collectives, per_device(): lax.psum(partial_mix, 'narrow')  24.5 us
    psum x1, blocking collectives, per_device(): lax.psum(partial_decay, 'narrow')  23.3 us
  transfers between devices with their start and end apart: 10, of which 7 were waited for; matrix products, arithmetic and copies ran while one was open for 5% of the time, Pallas kernels for 0%

profile of v1, /device:TPU:24, one launch (start us, length us, event | category | flops | bytes accessed | tf_op | source)
XLA Modules:
  0.0 1135.9 jit_solution(3230499768780510935)
XLA Ops:
  9.4 14.1 %all-reduce.2 = (f32[16,1]{0,1:T(1,128)S(1)}, f32[16,1]{0,1:T(1,128)S(1)}, f32[16,1]{0,1:T(1,128)S(1)}, f32[16,1]{0,1:T(1,128)S(1)}, f32[16,1]{0,1:T(1,128)S(1)}...) all-reduce(f32[16,1]{0,1:T(1,128)S(1)} %bitcast.886, ...), channel_id=1, replica_groups=mesh['wide'=64,'narrow'=8] {'narrow'}, use_global_device_ids=true, to_apply=%region_23.24 | all-reduce | flops 128 | bytes 1024 | tf_op jit(solution)/shard_map/psum | solution.py:49
  32.9 24.5 %all-reduce.1 = (f32[16,1,160]{2,0,1:T(8,128)S(1)}, f32[16,1,160]{2,0,1:T(8,128)S(1)}, f32[16,1,160]{2,0,1:T(8,128)S(1)}, f32[16,1,160]{2,0,1:T(8,128)S(1)}) all-reduce(f32[16,1,160]{2,0,1:T(8,128)S(1)} %convolution_bitcast_fusion, ...), channel_id=1, replica_groups=mesh['wide'=64,'narrow'=8] {'narrow'}, use_global_device_ids=true, to_apply=%region_34.35 | all-reduce | flops 10240 | bytes 81920 | tf_op jit(solution)/shard_map/psum | solution.py:68
  62.9 23.3 %all-reduce = (f32[16,1,64]{2,0,1:T(8,128)S(1)}, f32[16,1,64]{2,0,1:T(8,128)S(1)}, f32[16,1,64]{2,0,1:T(8,128)S(1)}, f32[16,1,64]{2,0,1:T(8,128)S(1)}) all-reduce(f32[16,1,64]{2,0,1:T(8,128)S(1)} %convolution_bitcast_fusion.4, f32[16,1,64]{2,0,1:T(8,128)S(1)} %convolution_bitcast_fusion.5, ...), channel_id=1, replica_groups=mesh['wide'=64,'narrow'=8] {'narrow'}, use_global_device_ids=true, to_apply=%region_35.36 | all-reduce | flops 4096 | bytes 32768 | tf_op jit(solution)/shard_map/psum | solution.py:84
  86.2 103.5 %all_gather.29 = bf16[1024,1,192]{2,0,1:T(8,128)(2,1)S(1)} all-gather(bf16[16,1,192]{2,0,1:T(8,128)(2,1)S(1)} %pad_maximum_fusion.1), channel_id=1, replica_groups=mesh['wide'=64,'narrow'=8] {'wide'}, dimensions={0}, use_global_device_ids=true | all-gather | bytes 399360 | tf_op jit(solution)/shard_map/all_gather | solution.py:87
  189.8 98.7 %all_gather.31 = bf16[1024,1,192]{2,0,1:T(8,128)(2,1)S(1)} all-gather(bf16[16,1,192]{2,0,1:T(8,128)(2,1)S(1)} %pad_maximum_fusion.2), channel_id=1, replica_groups=mesh['wide'=64,'narrow'=8] {'wide'}, dimensions={0}, use_global_device_ids=true | all-gather | bytes 399360 | tf_op jit(solution)/shard_map/all_gather | solution.py:87
  288.5 97.4 %all_gather.33 = bf16[1024,1,192]{2,0,1:T(8,128)(2,1)S(1)} all-gather(bf16[16,1,192]{2,0,1:T(8,128)(2,1)S(1)} %pad_maximum_fusion.3), channel_id=1, replica_groups=mesh['wide'=64,'narrow'=8] {'wide'}, dimensions={0}, use_global_device_ids=true | all-gather | bytes 399360 | tf_op jit(solution)/shard_map/all_gather | solution.py:87
  385.9 98.7 %all_gather.35 = bf16[1024,1,192]{2,0,1:T(8,128)(2,1)S(1)} all-gather(bf16[16,1,192]{2,0,1:T(8,128)(2,1)S(1)} %pad_maximum_fusion.4), channel_id=1, replica_groups=mesh['wide'=64,'narrow'=8] {'wide'}, dimensions={0}, use_global_device_ids=true | all-gather | bytes 399360 | tf_op jit(solution)/shard_map/all_gather | solution.py:87
  487.0 2.4 fusion.63
  489.5 2.4 fusion.62
  500.4 2.4 fusion.66
  502.8 2.4 fusion.65
  508.6 60.1 %all-gather.12.cloned.1.call-done = bf16[1024,1,512]{2,0,1:T(8,128)(2,1)} async-done(((bf16[16,1,512]{2,0,1:T(8,128)(2,1)}), bf16[1024,1,512]{2,0,1:T(8,128)(2,1)}) %all-gather.12.cloned.1.call-update) | async-done | bytes 1048592 | tf_op jit(solution)/shard_map/all_gather | solution.py:86
  571.0 2.4 fusion.70
  573.4 2.4 fusion.69
  579.2 127.3 %all-gather.14.cloned.1.call-done = bf16[1024,1,512]{2,0,1:T(8,128)(2,1)} async-done(((bf16[16,1,512]{2,0,1:T(8,128)(2,1)}), bf16[1024,1,512]{2,0,1:T(8,128)(2,1)}) %all-gather.14.cloned.1.call-update) | async-done | bytes 1048592 | tf_op jit(solution)/shard_map/all_gather | solution.py:86
  716.0 25.4 %reduce-scatter.13.cloned.1.call-done = bf16[128,256]{1,0:T(8,128)(2,1)} async-done(((bf16[1024,256]{1,0:T(8,128)(2,1)}), bf16[128,256]{1,0:T(8,128)(2,1)}) %reduce-scatter.13.cloned.1.call-update) | async-done | bytes 65552
  742.4 39.6 %reduce-scatter.15.cloned.1.call-done = bf16[128,256]{1,0:T(8,128)(2,1)} async-done(((bf16[1024,256]{1,0:T(8,128)(2,1)}), bf16[128,256]{1,0:T(8,128)(2,1)}) %reduce-scatter.15.cloned.1.call-update) | async-done | bytes 65552
  783.0 39.4 %reduce-scatter.17.cloned.1.call-done = bf16[128,256]{1,0:T(8,128)(2,1)} async-done(((bf16[1024,256]{1,0:T(8,128)(2,1)}), bf16[128,256]{1,0:T(8,128)(2,1)}) %reduce-scatter.17.cloned.1.call-update) | async-done | bytes 65552
  823.4 39.6 %reduce-scatter.19.cloned.1.call-done = bf16[128,256]{1,0:T(8,128)(2,1)} async-done(((bf16[1024,256]{1,0:T(8,128)(2,1)}), bf16[128,256]{1,0:T(8,128)(2,1)}) %reduce-scatter.19.cloned.1.call-update) | async-done | bytes 65552
  872.8 72.0 %all_to_all.20 = bf16[64,128,1,64]{1,3,2,0:T(8,128)(2,1)S(1)} all-to-all(bf16[64,128,1,64]{1,3,2,0:T(8,128)(2,1)S(1)} %stack.12), channel_id=1, replica_groups=mesh['wide'=64,'narrow'=8] {'wide'}, dimensions={0} | all-to-all | bytes 2097152 | tf_op jit(solution)/shard_map/all_to_all | solution.py:165
  945.0 60.6 %all_to_all.21 = bf16[64,128,1,64]{1,3,2,0:T(8,128)(2,1)S(1)} all-to-all(bf16[64,128,1,64]{1,3,2,0:T(8,128)(2,1)S(1)} %stack.13), channel_id=1, replica_groups=mesh['wide'=64,'narrow'=8] {'wide'}, dimensions={0} | all-to-all | bytes 2097152 | tf_op jit(solution)/shard_map/all_to_all | solution.py:165
  1005.9 60.4 %all_to_all.22 = bf16[64,128,1,64]{1,3,2,0:T(8,128)(2,1)} all-to-all(bf16[64,128,1,64]{1,3,2,0:T(8,128)(2,1)S(1)} %stack.14), channel_id=1, replica_groups=mesh['wide'=64,'narrow'=8] {'wide'}, dimensions={0} | all-to-all | bytes 2097152 | tf_op jit(solution)/shard_map/all_to_all | solution.py:165
  1067.5 6.1 all-to-all-start.3
  1075.2 52.0 %all-to-all-done.3 = bf16[64,128,1,64]{1,3,2,0:T(8,128)(2,1)} async-done(((bf16[64,128,1,64]{1,3,2,0:T(8,128)(2,1)}), bf16[64,128,1,64]{1,3,2,0:T(8,128)(2,1)}, u32[]{:S(2)}, u32[]{:S(2)}) %all-to-all-start.3) | async-done | bytes 1048608 | tf_op jit(solution)/shard_map/all_to_all | solution.py:165
  (175 shorter events, 64.3 us)
Async XLA Ops:
  7.2 1066.5 %copy-start = (bf16[4096,64]{0,1:T(8,128)(2,1)S(1)}, bf16[4096,64]{0,1:T(8,128)(2,1)}, u32[]{:S(2)}) copy-start(bf16[4096,64]{0,1:T(8,128)(2,1)} %param.34) | copy-start | bytes 1572868
  7.2 53.8 %copy-start.5 = (bf16[16,512]{1,0:T(8,128)(2,1)S(1)}, bf16[16,512]{1,0:T(8,128)(2,1)}, u32[]{:S(2)}) copy-start(bf16[16,512]{1,0:T(8,128)(2,1)} %param.20) | copy-start | bytes 49156
  7.2 52.7 %copy-start.3 = (bf16[512,64]{0,1:T(8,128)(2,1)S(1)}, bf16[512,64]{0,1:T(8,128)(2,1)}, u32[]{:S(2)}) copy-start(bf16[512,64]{0,1:T(8,128)(2,1)} %param.26) | copy-start | bytes 196612
  7.2 54.9 %copy-start.9 = (f32[64]{0:T(128)S(1)}, f32[64]{0:T(128)}, u32[]{:S(2)}) copy-start(f32[64]{0:T(128)} %param.29) | copy-start | bytes 772
  7.2 479.8 %all-gather.8.cloned.1.call-start = ((), (), s32[]{:S(2)}) async-start(), calls=%async_computation.9 | async-start | bytes 1064960 | tf_op jit(solution)/shard_map/all_gather | solution.py:36
  7.9 479.1 %all-gather.6.cloned.1.call-start = ((), (), s32[]{:S(2)}) async-start(), calls=%async_computation.8 | async-start | bytes 1064960 | tf_op jit(solution)/shard_map/all_gather | solution.py:86
  25.0 472.9 %all-gather.10.cloned.1.call-start = ((), (), s32[]{:S(2)}) async-start(), calls=%async_computation.10 | async-start | bytes 1064960 | tf_op jit(solution)/shard_map/all_gather | solution.py:86
  25.8 542.9 %all-gather.12.cloned.1.call-start = ((), (), s32[]{:S(2)}) async-start(), calls=%async_computation.11 | async-start | bytes 1064960 | tf_op jit(solution)/shard_map/all_gather | solution.py:86
  26.3 680.2 %all-gather.14.cloned.1.call-start = ((), (), s32[]{:S(2)}) async-start(), calls=%async_computation.12 | async-start | bytes 1064960 | tf_op jit(solution)/shard_map/all_gather | solution.py:86
  26.9 714.5 %reduce-scatter.13.cloned.1.call-start = ((), (), s32[]{:S(2)}) async-start(), calls=%async_computation.13 | async-start | bytes 589824
  86.2 399.2 %copy-start.4 = (bf16[64,64]{1,0:T(8,128)(2,1)S(1)}, bf16[64,64]{1,0:T(8,128)(2,1)}, u32[]{:S(2)}) copy-start(bf16[64,64]{1,0:T(8,128)(2,1)} %param.27) | copy-start | bytes 24580
  86.2 399.2 %copy-start.8 = (f32[64]{0:T(128)S(1)}, f32[64]{0:T(128)}, u32[]{:S(2)}) copy-start(f32[64]{0:T(128)} %param.28) | copy-start | bytes 772
  489.4 2.5 copy-start.6
  489.5 2.5 copy-start.12
  489.5 2.5 copy-start.20
  491.9 2.4 copy-start.11
  491.9 2.4 copy-start.22
  497.7 2.7 copy-start.13
  497.7 2.7 copy-start.19
  497.7 284.3 %reduce-scatter.15.cloned.1.call-start = ((), (), s32[]{:S(2)}) async-start(), calls=%async_computation.14 | async-start | bytes 589824
  508.6 313.8 %reduce-scatter.17.cloned.1.call-start = ((), (), s32[]{:S(2)}) async-start(), calls=%async_computation.15 | async-start | bytes 589824
  579.1 129.7 %copy-start.17 = (bf16[1024,1,512]{2,0,1:T(8,128)(2,1)S(1)}, bf16[1024,1,512]{2,0,1:T(8,128)(2,1)}, u32[]{:S(2)}) copy-start(bf16[1024,1,512]{2,0,1:T(8,128)(2,1)} %all-gather.12.cloned.1.call-done) | copy-start | bytes 3145732
  579.1 283.8 %reduce-scatter.19.cloned.1.call-start = ((), (), s32[]{:S(2)}) async-start(), calls=%async_computation.16 | async-start | bytes 589824
  1067.5 59.7 %all-to-all-start.3 = ((bf16[64,128,1,64]{1,3,2,0:T(8,128)(2,1)}), bf16[64,128,1,64]{1,3,2,0:T(8,128)(2,1)}, u32[]{:S(2)}, u32[]{:S(2)}) async-start(bf16[64,128,1,64]{1,3,2,0:T(8,128)(2,1)} %stack.15), calls=%async_computation.3 | async-start | bytes 2097152 | tf_op jit(solution)/shard_map/all_to_all | solution.py:165
  (10 other events, 18.5 us)
Sparse Core Ops, SparseCore 0:
  11.0 143.1 all-gather.7
  157.7 135.0 all-gather.5
  295.8 134.8 all-gather.9
  433.5 135.1 all-gather.11
  571.5 134.9 all-gather.13
  709.7 31.6 reduce-scatter.12
  744.4 37.5 reduce-scatter.14
  784.8 37.5 reduce-scatter.16
  825.4 37.5 reduce-scatter.18
